TPU v7x, 32 devices: a whole 2x2x4 slice. The times are simulated.
32 devices in a mesh: gx: 2 (over y), gy: 4 (over x, core), gz: 4 (over z).
Axes of the slice: x: 2, y: 2, z: 4, core: 2. Of those that a mesh axis runs over, the one named last changes fastest.
Arguments:
- direction: float32 [3, 32, 32, 512], P(None, 'gx', 'gy', 'gz'), may hold values from -6 to 6
- base_flow: bfloat16 [2, 3, 32, 32, 512], P(None, None, 'gx', 'gy', 'gz'), may hold values from -4 to 4
- local_inv: float32 [32, 16], P('gx'), may hold values from -1.5 to 1.5
- couple_in: float32 [4, 16], P('gx'), may hold values from -1.5 to 1.5
- couple_out: float32 [32, 2], P('gx'), may hold values from -4 to 4
- schur_inv: float32 [4, 4], replicated, may hold values from -3 to 3
- plane_x: int32 [8], replicated, may hold values from 0 to 31, as said below
- slot_plane: int32 [8], replicated, may hold values from 0 to 7, each once
- window_inv: float32 [8, 4, 4, 16, 16], P('gx', 'gy', 'gz'), may hold values from -4 to 20
Outputs:
- hess_vec: float32 [3, 32, 32, 512], P(None, 'gx', 'gy', 'gz')
Inputs may be any that keep to these rules, and one draw needn't show every extreme that they name: `plane_x`: each plane lies on a streamwise cell of the grid; the planes lie on distinct cells; at most 8 of them lie in the cells of one index d of gx (cells d*16 to d*16 + 15), and some index holds exactly 8.
All inputs are finite; a program needn't handle non-finite values.
Results may differ from a plain program's by a relative error of at most 0.0003.
Values sent between devices are 32-bit elements; how exact they have to be, the bound alone decides.
A program may use at most 64 MiB of HBM per device.

v0:
```python
import jax
import jax.numpy as jnp
from jax import lax
from jax.sharding import PartitionSpec as P

WIN = 8
time_step = 0.15
high = lax.Precision.HIGHEST


def extended(cells, sides, width, closed):
    for axis, dim in sides:
        count = lax.axis_size(axis)
        ends = count if closed else count - 1
        head = lax.slice_in_dim(cells, 0, width, axis=dim)
        tail = lax.slice_in_dim(cells, cells.shape[dim] - width, cells.shape[dim], axis=dim)
        cells = jnp.concatenate(
            [
                lax.ppermute(tail, axis, [(i, (i + 1) % count) for i in range(ends)]),
                cells,
                lax.ppermute(head, axis, [((i + 1) % count, i) for i in range(ends)]),
            ],
            axis=dim,
        )
    return cells


def stencil_x(field):
    length = field.shape[1]
    padded = extended(field, (("gx", 1),), 2, False)
    near_diff = padded[:, 3 : length + 3] - padded[:, 1 : length + 1]
    far_diff = padded[:, 4 : length + 4] - padded[:, 0:length]
    return 7.0 / 9.0 * near_diff + 1.0 / 36.0 * far_diff


def cross_padded(field):
    return extended(field, (("gy", 2), ("gz", 3)), 3, True)


def sixth_order(minus_one, plus_one, minus_two, plus_two, minus_three, plus_three):
    return (
        45.0 * (plus_one - minus_one) - 9.0 * (plus_two - minus_two) + (plus_three - minus_three)
    ) / 60.0


def along_y(padded):
    height = padded.shape[2] - 6
    middle = padded[:, :, :, 3 : padded.shape[3] - 3]

    def taken(offset):
        return middle[:, :, 3 + offset : 3 + offset + height]

    return sixth_order(taken(-1), taken(1), taken(-2), taken(2), taken(-3), taken(3))


def along_z(padded):
    breadth = padded.shape[3] - 6
    middle = padded[:, :, 3 : padded.shape[2] - 3, :]

    def taken(offset):
        return middle[:, :, :, 3 + offset : 3 + offset + breadth]

    return sixth_order(taken(-1), taken(1), taken(-2), taken(2), taken(-3), taken(3))


def interface_sum(edge_values, weight_cols):
    return jnp.einsum(
        "ma,mcyz->acyz",
        weight_cols,
        lax.all_gather(edge_values, "gx", axis=0, tiled=True),
        precision=high,
    )


def local(
    direction,
    base_flow,
    local_inv,
    couple_in,
    couple_out,
    schur_inv,
    plane_x,
    slot_plane,
    window_inv,
):
    gx_index = lax.axis_index("gx")
    holders = lax.axis_size("gx")
    x_cells = direction.shape[1]
    planes = plane_x.shape[0]
    owned_slots = window_inv.shape[0]
    window_count = window_inv.shape[3]
    hold_most = min(planes, 3 * owned_slots)
    own_rows = lax.dynamic_slice_in_dim(schur_inv, 2 * gx_index, 2, 0)
    own_cols = lax.dynamic_slice_in_dim(schur_inv, 2 * gx_index, 2, 1)

    def solve_x(rhs):
        local_part = jnp.einsum("ij,cjyz->ciyz", local_inv, rhs, precision=high)
        edge_values = jnp.einsum("kj,cjyz->kcyz", couple_in, rhs, precision=high)
        solved = interface_sum(edge_values, jnp.transpose(own_rows))
        return local_part + jnp.einsum("ik,kcyz->ciyz", couple_out, solved, precision=high)

    def solve_x_adjoint(grad_in):
        local_part = jnp.einsum("ji,cjyz->ciyz", local_inv, grad_in, precision=high)
        edge_values = jnp.einsum("ik,ciyz->kcyz", couple_out, grad_in, precision=high)
        solved = interface_sum(edge_values, own_cols)
        return local_part + jnp.einsum("ki,kcyz->ciyz", couple_in, solved, precision=high)

    owner_of = plane_x // x_cells
    device_hot = (owner_of[None, :] == jnp.arange(holders, dtype=jnp.int32)[:, None]).astype(
        jnp.int32
    )
    ranks = jnp.cumsum(device_hot, axis=1) - 1
    slot_range = jnp.arange(hold_most, dtype=jnp.int32)[None, :, None]
    pick_all = ((device_hot[:, None, :] == 1) & (ranks[:, None, :] == slot_range)).astype(
        jnp.float32
    )
    pick_own = lax.dynamic_index_in_dim(pick_all, gx_index, 0, keepdims=False)
    local_x = plane_x - gx_index * x_cells
    slot_x = jnp.sum(jnp.where(pick_own > 0, local_x[None, :], 0), axis=1)
    filled = jnp.sum(pick_own, axis=1) > 0
    cell_range = jnp.arange(x_cells, dtype=jnp.int32)[None, :]
    select = (filled[:, None] & (slot_x[:, None] == cell_range)).astype(jnp.float32)
    plane_slot = (slot_plane[:, None] == jnp.arange(planes, dtype=jnp.int32)[None, :]).astype(
        jnp.float32
    )
    route = jnp.dot(pick_own, jnp.transpose(plane_slot), precision=high)
    inverse_here = window_inv.reshape(owned_slots, window_count, window_count)

    def windows_of(state):
        plane_rows = jnp.einsum("sx,cxyz->scyz", select, state, precision=high)
        return plane_rows.reshape(
            plane_rows.shape[0], 3, plane_rows.shape[2], plane_rows.shape[3] // WIN, WIN
        ).mean(axis=4)

    def spread_back(weighted):
        expanded = jnp.repeat(weighted, WIN, axis=3) / WIN
        return jnp.einsum("sx,scyz->cxyz", select, expanded, precision=high)

    every_inv = lax.all_gather(inverse_here, "gx", axis=0, tiled=True)
    held_inv = jnp.einsum("sj,jab->sab", route, every_inv, precision=high)

    def observe(state):
        weighted = jnp.einsum("sab,scyb->scya", held_inv, windows_of(state), precision=high)
        return spread_back(weighted)

    def tangent(state, step_base):
        velocity = step_base.astype(jnp.float32)
        slope_x = solve_x(stencil_x(state))
        padded = cross_padded(state)
        return state - time_step * (
            velocity[0] * slope_x + velocity[1] * along_y(padded) + velocity[2] * along_z(padded)
        )

    def adjoint(state, step_base):
        velocity = step_base.astype(jnp.float32)
        pulled = stencil_x(solve_x_adjoint(velocity[0] * state))
        padded = cross_padded(jnp.concatenate([velocity[1] * state, velocity[2] * state], axis=0))
        return state + time_step * (pulled + along_y(padded[:3]) + along_z(padded[3:]))

    state_one = tangent(direction, base_flow[0])
    state_two = tangent(state_one, base_flow[1])
    adjoint_two = observe(state_two)
    adjoint_one = adjoint(adjoint_two, base_flow[1]) + observe(state_one)
    return adjoint(adjoint_one, base_flow[0]) + direction


def solution(mesh):
    return jax.shard_map(
        local,
        mesh=mesh,
        in_specs=(
            P(None, "gx", "gy", "gz"),
            P(None, None, "gx", "gy", "gz"),
            P("gx", None),
            P("gx", None),
            P("gx", None),
            P(),
            P(),
            P(),
            P("gx", "gy", "gz", None, None),
        ),
        out_specs=P(None, "gx", "gy", "gz"),
        check_vma=False,
    )
```

profile of v0, /device:TPU:0, one launch (start us, length us, event | category | flops | bytes accessed | tf_op | source)
XLA Modules:
  0.0 129.9 jit_solution(2365292226690273208)
XLA Ops:
  0.0 1.0 copy.84
  1.0 0.5 collective-permute-start.3
  1.6 2.0 %collective-permute-start.2 = (f32[3,16,3,128]{3,1,2,0:T(8,128)S(1)}, f32[3,16,3,128]{3,1,2,0:T(8,128)S(1)}, u32[]{:S(2)}, u32[]{:S(2)}) collective-permute-start(f32[3,16,3,128]{3,1,2,0:T(8,128)S(1)} %get-tuple-element.51), channel_id=1, source_target_pairs={{4,0},{8,4},{12,8},{0,12},{5,1},{9,5},{13,9},{1,13},{6,2},{10,6},{... | collective-permute-start | bytes 221192 | tf_op jit(solution)/shard_map/ppermute | solution.py:21
  3.6 4.2 %collective-permute-start.1 = (f32[3,2,8,128]{3,1,2,0:T(2,128)S(1)}, f32[3,2,8,128]{3,1,2,0:T(2,128)S(1)}, u32[]{:S(2)}, u32[]{:S(2)}) collective-permute-start(f32[3,2,8,128]{3,1,2,0:T(2,128)S(1)} %get-tuple-element.44), channel_id=1, source_target_pairs={{0,16},{1,17},{2,18},{3,19},{4,20},{5,21},{6,22},{7,23},{8,24},{9,... | collective-permute-start | bytes 73736 | tf_op jit(solution)/shard_map/ppermute | solution.py:19
  7.8 1.3 collective-permute-start
  9.1 1.0 slice_convert_fusion
  10.1 0.6 copy.110
  10.8 0.6 copy.111
  12.0 5.2 %all-gather = f32[8,1,1,16,16]{4,3,2,1,0:T(8,128)S(1)} all-gather(f32[4,1,1,16,16]{4,3,2,1,0:T(8,128)S(1)} %copy-done.4), channel_id=2, replica_groups=mesh['gx'=2,'gy'=4,'gz'=4] {'gx'}, dimensions={0}, use_global_device_ids=true | all-gather | bytes 12288 | tf_op jit(solution)/shard_map/all_gather | solution.py:139
  18.0 1.6 %collective-permute-start.5 = (f32[3,16,14,3]{3,1,2,0:T(8,128)S(1)}, f32[3,16,14,3]{3,1,2,0:T(8,128)S(1)}, u32[]{:S(2)}, u32[]{:S(2)}) collective-permute-start(f32[3,16,14,3]{3,1,2,0:T(8,128)S(1)} %get-tuple-element.20), channel_id=1, source_target_pairs={{0,1},{1,2},{2,3},{3,0},{4,5},{5,6},{6,7},{7,4},{8,9},{9,10},{10,1... | collective-permute-start | bytes 24200 | tf_op jit(solution)/shard_map/ppermute | solution.py:19
  19.6 2.2 %collective-permute-start.4 = (f32[3,16,14,3]{3,1,2,0:T(8,128)S(1)}, f32[3,16,14,3]{3,1,2,0:T(8,128)S(1)}, u32[]{:S(2)}, u32[]{:S(2)}) collective-permute-start(f32[3,16,14,3]{3,1,2,0:T(8,128)S(1)} %get-tuple-element.19), channel_id=1, source_target_pairs={{1,0},{2,1},{3,2},{0,3},{5,4},{6,5},{7,6},{4,7},{9,8},{10,9},{11,1... | collective-permute-start | bytes 24200 | tf_op jit(solution)/shard_map/ppermute | solution.py:21
  22.6 4.5 %all_gather.15 = f32[4,3,8,128]{3,2,1,0:T(8,128)S(1)} all-gather(f32[2,3,8,128]{3,2,1,0:T(8,128)S(1)} %copy.75), channel_id=1, replica_groups=mesh['gx'=2,'gy'=4,'gz'=4] {'gx'}, dimensions={0}, use_global_device_ids=true | all-gather | bytes 73728 | tf_op jit(solution)/shard_map/all_gather | solution.py:70
  27.3 3.5 %collective-permute-done.5 = f32[3,16,14,3]{3,1,2,0:T(8,128)S(1)} collective-permute-done((f32[3,16,14,3]{3,1,2,0:T(8,128)S(1)}, f32[3,16,14,3]{3,1,2,0:T(8,128)S(1)}, u32[]{:S(2)}, u32[]{:S(2)}) %collective-permute-start.5) | collective-permute-done | bytes 8096 | tf_op jit(solution)/shard_map/ppermute | solution.py:19
  30.8 4.3 %collective-permute-done.4 = f32[3,16,14,3]{3,1,2,0:T(8,128)S(1)} collective-permute-done((f32[3,16,14,3]{3,1,2,0:T(8,128)S(1)}, f32[3,16,14,3]{3,1,2,0:T(8,128)S(1)}, u32[]{:S(2)}, u32[]{:S(2)}) %collective-permute-start.4) | collective-permute-done | bytes 8096 | tf_op jit(solution)/shard_map/ppermute | solution.py:21
  35.1 0.8 fusion.90
  36.2 0.8 reshape.79
  37.0 3.7 %collective-permute-start.7 = (f32[3,2,8,128]{3,1,2,0:T(2,128)S(1)}, f32[3,2,8,128]{3,1,2,0:T(2,128)S(1)}, u32[]{:S(2)}, u32[]{:S(2)}) collective-permute-start(f32[3,2,8,128]{3,1,2,0:T(2,128)S(1)} %get-tuple-element.42), channel_id=1, source_target_pairs={{0,16},{1,17},{2,18},{3,19},{4,20},{5,21},{6,22},{7,23},{8,24},{9,... | collective-permute-start | bytes 73736 | tf_op jit(solution)/shard_map/ppermute | solution.py:19
  40.7 1.3 collective-permute-start.6
  42.0 0.5 reduce_sum.39
  42.8 0.5 broadcast_in_dim.19
  43.3 0.8 div.55
  44.1 1.7 %collective-permute-start.8 = (f32[3,16,3,128]{3,1,2,0:T(8,128)S(1)}, f32[3,16,3,128]{3,1,2,0:T(8,128)S(1)}, u32[]{:S(2)}, u32[]{:S(2)}) collective-permute-start(f32[3,16,3,128]{3,1,2,0:T(8,128)S(1)} %get-tuple-element.37), channel_id=1, source_target_pairs={{4,0},{8,4},{12,8},{0,12},{5,1},{9,5},{13,9},{1,13},{6,2},{10,6},{... | collective-permute-start | bytes 221192 | tf_op jit(solution)/shard_map/ppermute | solution.py:21
  45.8 0.6 collective-permute-done.6
  47.1 4.5 %all_gather.16 = f32[4,3,8,128]{3,2,1,0:T(8,128)S(1)} all-gather(f32[2,3,8,128]{3,2,1,0:T(8,128)S(1)} %copy.86), channel_id=1, replica_groups=mesh['gx'=2,'gy'=4,'gz'=4] {'gx'}, dimensions={0}, use_global_device_ids=true | all-gather | bytes 73728 | tf_op jit(solution)/shard_map/all_gather | solution.py:70
  52.1 1.2 collective-permute-start.11
  53.3 2.7 %collective-permute-start.10 = (f32[3,16,14,3]{3,1,2,0:T(8,128)S(1)}, f32[3,16,14,3]{3,1,2,0:T(8,128)S(1)}, u32[]{:S(2)}, u32[]{:S(2)}) collective-permute-start(f32[3,16,14,3]{3,1,2,0:T(8,128)S(1)} %get-tuple-element.17), channel_id=1, source_target_pairs={{1,0},{2,1},{3,2},{0,3},{5,4},{6,5},{7,6},{4,7},{9,8},{10,9},{11,1... | collective-permute-start | bytes 24200 | tf_op jit(solution)/shard_map/ppermute | solution.py:21
  56.3 8.5 %collective-permute-done.11 = f32[3,16,14,3]{3,1,2,0:T(8,128)S(1)} collective-permute-done((f32[3,16,14,3]{3,1,2,0:T(8,128)S(1)}, f32[3,16,14,3]{3,1,2,0:T(8,128)S(1)}, u32[]{:S(2)}, u32[]{:S(2)}) %collective-permute-start.11) | collective-permute-done | bytes 8096 | tf_op jit(solution)/shard_map/ppermute | solution.py:19
  64.9 3.5 %collective-permute-done.10 = f32[3,16,14,3]{3,1,2,0:T(8,128)S(1)} collective-permute-done((f32[3,16,14,3]{3,1,2,0:T(8,128)S(1)}, f32[3,16,14,3]{3,1,2,0:T(8,128)S(1)}, u32[]{:S(2)}, u32[]{:S(2)}) %collective-permute-start.10) | collective-permute-done | bytes 8096 | tf_op jit(solution)/shard_map/ppermute | solution.py:21
  68.4 0.8 fusion.102
  69.2 0.8 reshape.77
  70.0 0.5 reduce_sum.38
  70.8 0.5 broadcast_in_dim.18
  71.3 0.8 div.50
  72.1 0.4 broadcast_multiply_fusion.3
  73.7 4.6 %all_gather.18 = f32[4,3,8,128]{3,2,1,0:T(8,128)S(1)} all-gather(f32[2,3,8,128]{3,2,1,0:T(8,128)S(1)} %copy.96), channel_id=1, replica_groups=mesh['gx'=2,'gy'=4,'gz'=4] {'gx'}, dimensions={0}, use_global_device_ids=true | all-gather | bytes 73728 | tf_op jit(solution)/shard_map/all_gather | solution.py:70
  78.6 0.4 fusion.4
  79.0 3.7 %collective-permute-start.13 = (f32[3,2,8,128]{3,1,2,0:T(2,128)S(1)}, f32[3,2,8,128]{3,1,2,0:T(2,128)S(1)}, u32[]{:S(2)}, u32[]{:S(2)}) collective-permute-start(f32[3,2,8,128]{3,1,2,0:T(2,128)S(1)} %get-tuple-element.34), channel_id=1, source_target_pairs={{0,16},{1,17},{2,18},{3,19},{4,20},{5,21},{6,22},{7,23},{8,24},{9,... | collective-permute-start | bytes 73736 | tf_op jit(solution)/shard_map/ppermute | solution.py:19
  82.6 1.3 collective-permute-start.12
  84.3 0.7 copy.102
  85.0 1.0 collective-permute-start.17
  86.0 0.7 copy.100
  86.7 3.1 %collective-permute-start.16 = (f32[6,16,14,3]{2,1,3,0:T(8,128)S(1)}, f32[6,16,14,3]{2,1,3,0:T(8,128)}, u32[]{:S(2)}, u32[]{:S(2)}) collective-permute-start(f32[6,16,14,3]{2,1,3,0:T(8,128)S(1)} %copy.100), channel_id=1, source_target_pairs={{1,0},{2,1},{3,2},{0,3},{5,4},{6,5},{7,6},{4,7},{9,8},{10,9},{11,1... | collective-permute-start | bytes 48392 | tf_op jit(solution)/shard_map/ppermute | solution.py:21
  89.8 1.1 pad_maximum_fusion.2
  90.9 2.9 %collective-permute-done.17 = f32[6,16,14,3]{2,1,3,0:T(8,128)S(1)} collective-permute-done((f32[6,16,14,3]{2,1,3,0:T(8,128)S(1)}, f32[6,16,14,3]{2,1,3,0:T(8,128)S(1)}, u32[]{:S(2)}, u32[]{:S(2)}) %collective-permute-start.17) | collective-permute-done | bytes 16160 | tf_op jit(solution)/shard_map/ppermute | solution.py:19
  93.8 0.8 copy.103
  94.5 1.0 collective-permute-done.16
  95.5 1.7 %copy.101 = f32[6,16,14,3]{3,1,2,0:T(8,128)S(1)} copy(f32[6,16,14,3]{2,1,3,0:T(8,128)} %collective-permute-done.16) | data formatting | bytes 32256 | tf_op jit(solution)/shard_map/ppermute | solution.py:21
  97.2 0.6 copy-done.14
  97.8 2.1 %broadcast_multiply_fusion.1 = (f32[3,16,8,128]{3,1,2,0:T(8,128)S(1)}, f32[3,16,8,128]{3,1,2,0:T(8,128)S(1)}, f32[3,16,8,128]{3,1,2,0:T(8,128)S(1)}) fusion(f32[16,8,128]{2,0,1:T(8,128)S(1)} %copy-done.3, f32[16,8,128]{2,0,1:T(8,128)} %copy.111, s32[8]{0:T(128)S(1)} %copy-done.10, pred[8]{0:T(512)(128)(4,1)S(1)} %copy-done.12, ...), kind=kOutput, calls=%fused_computation.209 | convolution fusion | flops 7471360 | bytes 3161640 | tf_op jit(solution)/shard_map/sx,scyz->cxyz/dot_general | solution.py:137
  100.6 4.8 %all_gather.19 = f32[4,3,8,128]{3,2,1,0:T(8,128)S(1)} all-gather(f32[2,3,8,128]{3,2,1,0:T(8,128)S(1)} %copy.108), channel_id=1, replica_groups=mesh['gx'=2,'gy'=4,'gz'=4] {'gx'}, dimensions={0}, use_global_device_ids=true | all-gather | bytes 73728 | tf_op jit(solution)/shard_map/all_gather | solution.py:70
  105.8 0.5 collective-permute-start.21
  106.7 0.7 fusion.180
  107.4 4.5 %collective-permute-start.19 = (f32[3,2,8,128]{3,1,2,0:T(2,128)}, f32[3,2,8,128]{3,1,2,0:T(2,128)}, u32[]{:S(2)}, u32[]{:S(2)}) collective-permute-start(f32[3,2,8,128]{3,1,2,0:T(2,128)} %get-tuple-element.27), channel_id=1, source_target_pairs={{0,16},{1,17},{2,18},{3,19},{4,20},{5,21},{6,22},{7,23},{8,24},{9,... | collective-permute-start | bytes 73736 | tf_op jit(solution)/shard_map/ppermute | solution.py:19
  111.9 1.3 collective-permute-start.18
  113.6 1.4 %copy.114 = f32[6,16,14,3]{2,1,3,0:T(8,128)} copy(f32[6,16,14,3]{3,1,2,0:T(8,128)S(1)} %get-tuple-element.6) | data formatting | bytes 32256 | tf_op jit(solution)/shard_map/slice | solution.py:16
  115.0 1.1 collective-permute-start.23
  116.1 0.7 copy.112
  116.8 2.8 %collective-permute-start.22 = (f32[6,16,14,3]{2,1,3,0:T(8,128)S(1)}, f32[6,16,14,3]{2,1,3,0:T(8,128)}, u32[]{:S(2)}, u32[]{:S(2)}) collective-permute-start(f32[6,16,14,3]{2,1,3,0:T(8,128)S(1)} %copy.112), channel_id=1, source_target_pairs={{1,0},{2,1},{3,2},{0,3},{5,4},{6,5},{7,6},{4,7},{9,8},{10,9},{11,1... | collective-permute-start | bytes 48392 | tf_op jit(solution)/shard_map/ppermute | solution.py:21
  119.6 4.1 %collective-permute-done.23 = f32[6,16,14,3]{2,1,3,0:T(8,128)S(1)} collective-permute-done((f32[6,16,14,3]{2,1,3,0:T(8,128)}, f32[6,16,14,3]{2,1,3,0:T(8,128)S(1)}, u32[]{:S(2)}, u32[]{:S(2)}) %collective-permute-start.23) | collective-permute-done | bytes 16160 | tf_op jit(solution)/shard_map/ppermute | solution.py:19
  123.7 0.8 copy.115
  124.5 1.0 collective-permute-done.22
  125.5 1.7 %copy.113 = f32[6,16,14,3]{3,1,2,0:T(8,128)S(1)} copy(f32[6,16,14,3]{2,1,3,0:T(8,128)} %collective-permute-done.22) | data formatting | bytes 32256 | tf_op jit(solution)/shard_map/ppermute | solution.py:21
  127.2 1.9 %fusion.30 = f32[3,16,8,128]{3,1,2,0:T(8,128)S(1)} fusion(f32[3,16,8,128]{3,1,2,0:T(8,128)S(1)} %get-tuple-element.62, f32[3,2,8,128]{3,1,2,0:T(2,128)} %collective-permute-done.19, f32[3,16,8,128]{3,1,2,0:T(8,128)} %copy-done.2, f32[3,2,8,128]{3,1,2,0:T(2,128)} %collective-permute-done.18, f32[6,16,14,3]{3,1,2,0:T(8,128)S(1)} %copy.115, ...), kind=kLoop, calls=%fused_computation.73 | loop fusion | flops 2654208 | bytes 2735616 | tf_op jit(solution)/shard_map/add | solution.py:164
  129.1 0.7 copy.117
  (116 shorter events, 8.3 us)
Async XLA Ops:
  0.0 22.0 %copy-start = (f32[16,16]{1,0:T(8,128)S(1)}, f32[16,16]{1,0:T(8,128)}, u32[]{:S(2)}) copy-start(f32[16,16]{1,0:T(8,128)} %param.11) | copy-start | bytes 3076
  0.0 11.4 %copy-start.13 = (s32[8]{0:T(128)S(1)}, s32[8]{0:T(128)}, u32[]{:S(2)}) copy-start(s32[8]{0:T(128)} %param.15) | copy-start | bytes 100
  1.0 10.8 %copy-start.16 = (s32[8]{0:T(128)S(1)}, s32[8]{0:T(128)}, u32[]{:S(2)}) copy-start(s32[8]{0:T(128)} %param.16) | copy-start | bytes 100
  1.0 11.0 %copy-start.4 = (f32[4,1,1,16,16]{4,3,2,1,0:T(8,128)S(1)}, f32[4,1,1,16,16]{4,3,2,1,0:T(8,128)}, u32[]{:S(2)}) copy-start(f32[4,1,1,16,16]{4,3,2,1,0:T(8,128)} %param.17) | copy-start | bytes 12292
  1.0 16.6 %collective-permute-start.3 = (f32[3,16,3,128]{3,1,2,0:T(8,128)S(1)}, f32[3,16,3,128]{3,1,2,0:T(8,128)S(1)}, u32[]{:S(2)}, u32[]{:S(2)}) collective-permute-start(f32[3,16,3,128]{3,1,2,0:T(8,128)S(1)} %get-tuple-element.52), channel_id=1, source_target_pairs={{0,4},{4,8},{8,12},{12,0},{1,5},{5,9},{9,13},{13,1},{2,6},{6,10},{... | collective-permute-start | bytes 221192 | tf_op jit(solution)/shard_map/ppermute | solution.py:19
  1.6 16.2 %collective-permute-start.2 = (f32[3,16,3,128]{3,1,2,0:T(8,128)S(1)}, f32[3,16,3,128]{3,1,2,0:T(8,128)S(1)}, u32[]{:S(2)}, u32[]{:S(2)}) collective-permute-start(f32[3,16,3,128]{3,1,2,0:T(8,128)S(1)} %get-tuple-element.51), channel_id=1, source_target_pairs={{4,0},{8,4},{12,8},{0,12},{5,1},{9,5},{13,9},{1,13},{6,2},{10,6},{... | collective-permute-start | bytes 221192 | tf_op jit(solution)/shard_map/ppermute | solution.py:21
  3.6 18.3 %collective-permute-start.1 = (f32[3,2,8,128]{3,1,2,0:T(2,128)S(1)}, f32[3,2,8,128]{3,1,2,0:T(2,128)S(1)}, u32[]{:S(2)}, u32[]{:S(2)}) collective-permute-start(f32[3,2,8,128]{3,1,2,0:T(2,128)S(1)} %get-tuple-element.44), channel_id=1, source_target_pairs={{0,16},{1,17},{2,18},{3,19},{4,20},{5,21},{6,22},{7,23},{8,24},{9,... | collective-permute-start | bytes 73736 | tf_op jit(solution)/shard_map/ppermute | solution.py:19
  7.8 14.1 %collective-permute-start = (f32[3,2,8,128]{3,1,2,0:T(2,128)S(1)}, f32[3,2,8,128]{3,1,2,0:T(2,128)S(1)}, u32[]{:S(2)}, u32[]{:S(2)}) collective-permute-start(f32[3,2,8,128]{3,1,2,0:T(2,128)S(1)} %get-tuple-element.43), channel_id=1, source_target_pairs={{16,0},{17,1},{18,2},{19,3},{20,4},{21,5},{22,6},{23,7},{24,8},{25... | collective-permute-start | bytes 73736 | tf_op jit(solution)/shard_map/ppermute | solution.py:21
  10.0 7.6 %copy-start.1 = (f32[3,16,8,128]{3,2,1,0:T(8,128)S(1)}, f32[3,16,8,128]{3,2,1,0:T(8,128)}, u32[]{:S(2)}) copy-start(f32[3,16,8,128]{3,2,1,0:T(8,128)} %param.9) | copy-start | bytes 589828
  11.8 60.3 %copy-start.11 = (pred[8]{0:T(512)(128)(4,1)}, pred[8]{0:T(512)(128)(4,1)S(1)}, u32[]{:S(2)}) copy-start(pred[8]{0:T(512)(128)(4,1)S(1)} %broadcast_compare_fusion.1) | copy-start | bytes 28
  17.6 54.4 %copy-start.9 = (s32[8]{0:T(128)}, s32[8]{0:T(128)S(1)}, u32[]{:S(2)}) copy-start(s32[8]{0:T(128)S(1)} %select_reduce_fusion) | copy-start | bytes 100
  17.7 4.6 %copy-start.7 = (f32[2,16]{1,0:T(2,128)S(1)}, f32[2,16]{1,0:T(2,128)}, u32[]{:S(2)}) copy-start(f32[2,16]{1,0:T(2,128)} %param.12) | copy-start | bytes 388
  17.8 9.3 %copy-start.5 = (f32[4,4]{1,0:T(4,128)S(1)}, f32[4,4]{1,0:T(4,128)}, u32[]{:S(2)}) copy-start(f32[4,4]{1,0:T(4,128)} %param.14) | copy-start | bytes 196
  17.8 17.3 %copy-start.6 = (f32[16,2]{0,1:T(2,128)S(1)}, f32[16,2]{0,1:T(2,128)}, u32[]{:S(2)}) copy-start(f32[16,2]{0,1:T(2,128)} %param.13) | copy-start | bytes 388
  18.0 12.8 %collective-permute-start.5 = (f32[3,16,14,3]{3,1,2,0:T(8,128)S(1)}, f32[3,16,14,3]{3,1,2,0:T(8,128)S(1)}, u32[]{:S(2)}, u32[]{:S(2)}) collective-permute-start(f32[3,16,14,3]{3,1,2,0:T(8,128)S(1)} %get-tuple-element.20), channel_id=1, source_target_pairs={{0,1},{1,2},{2,3},{3,0},{4,5},{5,6},{6,7},{7,4},{8,9},{9,10},{10,1... | collective-permute-start | bytes 24200 | tf_op jit(solution)/shard_map/ppermute | solution.py:19
  19.6 15.5 %collective-permute-start.4 = (f32[3,16,14,3]{3,1,2,0:T(8,128)S(1)}, f32[3,16,14,3]{3,1,2,0:T(8,128)S(1)}, u32[]{:S(2)}, u32[]{:S(2)}) collective-permute-start(f32[3,16,14,3]{3,1,2,0:T(8,128)S(1)} %get-tuple-element.19), channel_id=1, source_target_pairs={{1,0},{2,1},{3,2},{0,3},{5,4},{6,5},{7,6},{4,7},{9,8},{10,9},{11,1... | collective-permute-start | bytes 24200 | tf_op jit(solution)/shard_map/ppermute | solution.py:21
  37.0 8.8 %collective-permute-start.7 = (f32[3,2,8,128]{3,1,2,0:T(2,128)S(1)}, f32[3,2,8,128]{3,1,2,0:T(2,128)S(1)}, u32[]{:S(2)}, u32[]{:S(2)}) collective-permute-start(f32[3,2,8,128]{3,1,2,0:T(2,128)S(1)} %get-tuple-element.42), channel_id=1, source_target_pairs={{0,16},{1,17},{2,18},{3,19},{4,20},{5,21},{6,22},{7,23},{8,24},{9,... | collective-permute-start | bytes 73736 | tf_op jit(solution)/shard_map/ppermute | solution.py:19
  40.7 5.7 %collective-permute-start.6 = (f32[3,2,8,128]{3,1,2,0:T(2,128)S(1)}, f32[3,2,8,128]{3,1,2,0:T(2,128)S(1)}, u32[]{:S(2)}, u32[]{:S(2)}) collective-permute-start(f32[3,2,8,128]{3,1,2,0:T(2,128)S(1)} %get-tuple-element.41), channel_id=1, source_target_pairs={{16,0},{17,1},{18,2},{19,3},{20,4},{21,5},{22,6},{23,7},{24,8},{25... | collective-permute-start | bytes 73736 | tf_op jit(solution)/shard_map/ppermute | solution.py:21
  44.0 7.8 %collective-permute-start.9 = (f32[3,16,3,128]{3,1,2,0:T(8,128)S(1)}, f32[3,16,3,128]{3,1,2,0:T(8,128)S(1)}, u32[]{:S(2)}, u32[]{:S(2)}) collective-permute-start(f32[3,16,3,128]{3,1,2,0:T(8,128)S(1)} %get-tuple-element.38), channel_id=1, source_target_pairs={{0,4},{4,8},{8,12},{12,0},{1,5},{5,9},{9,13},{13,1},{2,6},{6,10},{... | collective-permute-start | bytes 221192 | tf_op jit(solution)/shard_map/ppermute | solution.py:19
  44.1 7.8 %collective-permute-start.8 = (f32[3,16,3,128]{3,1,2,0:T(8,128)S(1)}, f32[3,16,3,128]{3,1,2,0:T(8,128)S(1)}, u32[]{:S(2)}, u32[]{:S(2)}) collective-permute-start(f32[3,16,3,128]{3,1,2,0:T(8,128)S(1)} %get-tuple-element.37), channel_id=1, source_target_pairs={{4,0},{8,4},{12,8},{0,12},{5,1},{9,5},{13,9},{1,13},{6,2},{10,6},{... | collective-permute-start | bytes 221192 | tf_op jit(solution)/shard_map/ppermute | solution.py:21
  52.1 12.8 %collective-permute-start.11 = (f32[3,16,14,3]{3,1,2,0:T(8,128)S(1)}, f32[3,16,14,3]{3,1,2,0:T(8,128)S(1)}, u32[]{:S(2)}, u32[]{:S(2)}) collective-permute-start(f32[3,16,14,3]{3,1,2,0:T(8,128)S(1)} %get-tuple-element.18), channel_id=1, source_target_pairs={{0,1},{1,2},{2,3},{3,0},{4,5},{5,6},{6,7},{7,4},{8,9},{9,10},{10,1... | collective-permute-start | bytes 24200 | tf_op jit(solution)/shard_map/ppermute | solution.py:19
  53.3 15.1 %collective-permute-start.10 = (f32[3,16,14,3]{3,1,2,0:T(8,128)S(1)}, f32[3,16,14,3]{3,1,2,0:T(8,128)S(1)}, u32[]{:S(2)}, u32[]{:S(2)}) collective-permute-start(f32[3,16,14,3]{3,1,2,0:T(8,128)S(1)} %get-tuple-element.17), channel_id=1, source_target_pairs={{1,0},{2,1},{3,2},{0,3},{5,4},{6,5},{7,6},{4,7},{9,8},{10,9},{11,1... | collective-permute-start | bytes 24200 | tf_op jit(solution)/shard_map/ppermute | solution.py:21
  73.1 10.8 %collective-permute-start.14 = (f32[6,16,3,128]{3,1,2,0:T(8,128)S(1)}, f32[6,16,3,128]{3,1,2,0:T(8,128)S(1)}, u32[]{:S(2)}, u32[]{:S(2)}) collective-permute-start(f32[6,16,3,128]{3,1,2,0:T(8,128)S(1)} %get-tuple-element.16), channel_id=1, source_target_pairs={{4,0},{8,4},{12,8},{0,12},{5,1},{9,5},{13,9},{1,13},{6,2},{10,6},{... | collective-permute-start | bytes 442376 | tf_op jit(solution)/shard_map/ppermute | solution.py:21
  73.3 10.6 %collective-permute-start.15 = (f32[6,16,3,128]{3,1,2,0:T(8,128)S(1)}, f32[6,16,3,128]{3,1,2,0:T(8,128)S(1)}, u32[]{:S(2)}, u32[]{:S(2)}) collective-permute-start(f32[6,16,3,128]{3,1,2,0:T(8,128)S(1)} %get-tuple-element.15), channel_id=1, source_target_pairs={{0,4},{4,8},{8,12},{12,0},{1,5},{5,9},{9,13},{13,1},{2,6},{6,10},{... | collective-permute-start | bytes 442376 | tf_op jit(solution)/shard_map/ppermute | solution.py:19
  79.0 18.2 %collective-permute-start.13 = (f32[3,2,8,128]{3,1,2,0:T(2,128)S(1)}, f32[3,2,8,128]{3,1,2,0:T(2,128)S(1)}, u32[]{:S(2)}, u32[]{:S(2)}) collective-permute-start(f32[3,2,8,128]{3,1,2,0:T(2,128)S(1)} %get-tuple-element.34), channel_id=1, source_target_pairs={{0,16},{1,17},{2,18},{3,19},{4,20},{5,21},{6,22},{7,23},{8,24},{9,... | collective-permute-start | bytes 73736 | tf_op jit(solution)/shard_map/ppermute | solution.py:19
  82.6 14.5 %collective-permute-start.12 = (f32[3,2,8,128]{3,1,2,0:T(2,128)S(1)}, f32[3,2,8,128]{3,1,2,0:T(2,128)S(1)}, u32[]{:S(2)}, u32[]{:S(2)}) collective-permute-start(f32[3,2,8,128]{3,1,2,0:T(2,128)S(1)} %get-tuple-element.33), channel_id=1, source_target_pairs={{16,0},{17,1},{18,2},{19,3},{20,4},{21,5},{22,6},{23,7},{24,8},{25... | collective-permute-start | bytes 73736 | tf_op jit(solution)/shard_map/ppermute | solution.py:21
  85.0 8.8 %collective-permute-start.17 = (f32[6,16,14,3]{2,1,3,0:T(8,128)S(1)}, f32[6,16,14,3]{2,1,3,0:T(8,128)S(1)}, u32[]{:S(2)}, u32[]{:S(2)}) collective-permute-start(f32[6,16,14,3]{2,1,3,0:T(8,128)S(1)} %copy.102), channel_id=1, source_target_pairs={{0,1},{1,2},{2,3},{3,0},{4,5},{5,6},{6,7},{7,4},{8,9},{9,10},{10,1... | collective-permute-start | bytes 48392 | tf_op jit(solution)/shard_map/ppermute | solution.py:19
  86.7 11.1 %copy-start.3 = (f32[16,8,128]{2,0,1:T(8,128)S(1)}, f32[16,8,128]{2,0,1:T(8,128)}, u32[]{:S(2)}) copy-start(f32[16,8,128]{2,0,1:T(8,128)} %copy.110) | copy-start | bytes 196612
  86.7 11.1 %copy-start.10 = (s32[8]{0:T(128)S(1)}, s32[8]{0:T(128)}, u32[]{:S(2)}) copy-start(s32[8]{0:T(128)} %copy-done.9) | copy-start | bytes 100
  86.7 11.1 %copy-start.12 = (pred[8]{0:T(512)(128)(4,1)S(1)}, pred[8]{0:T(512)(128)(4,1)}, u32[]{:S(2)}) copy-start(pred[8]{0:T(512)(128)(4,1)} %copy-done.11) | copy-start | bytes 28
  86.7 8.8 %collective-permute-start.16 = (f32[6,16,14,3]{2,1,3,0:T(8,128)S(1)}, f32[6,16,14,3]{2,1,3,0:T(8,128)}, u32[]{:S(2)}, u32[]{:S(2)}) collective-permute-start(f32[6,16,14,3]{2,1,3,0:T(8,128)S(1)} %copy.100), channel_id=1, source_target_pairs={{1,0},{2,1},{3,2},{0,3},{5,4},{6,5},{7,6},{4,7},{9,8},{10,9},{11,1... | collective-permute-start | bytes 48392 | tf_op jit(solution)/shard_map/ppermute | solution.py:21
  97.2 0.6 copy-start.14
  97.2 0.6 copy-start.15
  100.0 6.4 %copy-start.8 = (f32[2,16]{1,0:T(2,128)S(1)}, f32[2,16]{1,0:T(2,128)}, u32[]{:S(2)}) copy-start(f32[2,16]{1,0:T(2,128)} %param.12) | copy-start | bytes 388
  105.8 7.4 %collective-permute-start.20 = (f32[6,16,3,128]{3,1,2,0:T(8,128)S(1)}, f32[6,16,3,128]{3,1,2,0:T(8,128)S(1)}, u32[]{:S(2)}, u32[]{:S(2)}) collective-permute-start(f32[6,16,3,128]{3,1,2,0:T(8,128)S(1)} %get-tuple-element.12), channel_id=1, source_target_pairs={{4,0},{8,4},{12,8},{0,12},{5,1},{9,5},{13,9},{1,13},{6,2},{10,6},{... | collective-permute-start | bytes 442376 | tf_op jit(solution)/shard_map/ppermute | solution.py:21
  105.8 7.4 %collective-permute-start.21 = (f32[6,16,3,128]{3,1,2,0:T(8,128)S(1)}, f32[6,16,3,128]{3,1,2,0:T(8,128)S(1)}, u32[]{:S(2)}, u32[]{:S(2)}) collective-permute-start(f32[6,16,3,128]{3,1,2,0:T(8,128)S(1)} %get-tuple-element.11), channel_id=1, source_target_pairs={{0,4},{4,8},{8,12},{12,0},{1,5},{5,9},{9,13},{13,1},{2,6},{6,10},{... | collective-permute-start | bytes 442376 | tf_op jit(solution)/shard_map/ppermute | solution.py:19
  106.7 10.1 %copy-start.2 = (f32[3,16,8,128]{3,1,2,0:T(8,128)}, f32[3,16,8,128]{3,1,2,0:T(8,128)S(1)}, u32[]{:S(2)}) copy-start(f32[3,16,8,128]{3,1,2,0:T(8,128)S(1)} %fusion.5) | copy-start | bytes 589828
  107.4 19.8 %collective-permute-start.19 = (f32[3,2,8,128]{3,1,2,0:T(2,128)}, f32[3,2,8,128]{3,1,2,0:T(2,128)}, u32[]{:S(2)}, u32[]{:S(2)}) collective-permute-start(f32[3,2,8,128]{3,1,2,0:T(2,128)} %get-tuple-element.27), channel_id=1, source_target_pairs={{0,16},{1,17},{2,18},{3,19},{4,20},{5,21},{6,22},{7,23},{8,24},{9,... | collective-permute-start | bytes 73736 | tf_op jit(solution)/shard_map/ppermute | solution.py:19
  111.9 15.3 %collective-permute-start.18 = (f32[3,2,8,128]{3,1,2,0:T(2,128)}, f32[3,2,8,128]{3,1,2,0:T(2,128)}, u32[]{:S(2)}, u32[]{:S(2)}) collective-permute-start(f32[3,2,8,128]{3,1,2,0:T(2,128)} %get-tuple-element.26), channel_id=1, source_target_pairs={{16,0},{17,1},{18,2},{19,3},{20,4},{21,5},{22,6},{23,7},{24,8},{25... | collective-permute-start | bytes 73736 | tf_op jit(solution)/shard_map/ppermute | solution.py:21
  115.0 8.8 %collective-permute-start.23 = (f32[6,16,14,3]{2,1,3,0:T(8,128)}, f32[6,16,14,3]{2,1,3,0:T(8,128)S(1)}, u32[]{:S(2)}, u32[]{:S(2)}) collective-permute-start(f32[6,16,14,3]{2,1,3,0:T(8,128)} %copy.114), channel_id=1, source_target_pairs={{0,1},{1,2},{2,3},{3,0},{4,5},{5,6},{6,7},{7,4},{8,9},{9,10},{10,1... | collective-permute-start | bytes 48392 | tf_op jit(solution)/shard_map/ppermute | solution.py:19
  116.8 8.7 %collective-permute-start.22 = (f32[6,16,14,3]{2,1,3,0:T(8,128)S(1)}, f32[6,16,14,3]{2,1,3,0:T(8,128)}, u32[]{:S(2)}, u32[]{:S(2)}) collective-permute-start(f32[6,16,14,3]{2,1,3,0:T(8,128)S(1)} %copy.112), channel_id=1, source_target_pairs={{1,0},{2,1},{3,2},{0,3},{5,4},{6,5},{7,6},{4,7},{9,8},{10,9},{11,1... | collective-permute-start | bytes 48392 | tf_op jit(solution)/shard_map/ppermute | solution.py:21
where the time goes:
time: 130 us
  starting transfers between devices  42.3 us (33%)
  waiting for transfers between devices  29.4 us (23%)
  blocking collectives  23.5 us (18%)
  local copies, waits for them, and re-layouts  18.1 us (14%)
  matrix products  9.75 us (8%)
  other arithmetic  5.91 us (5%)
    ppermute x12, starting transfers between devices, extended(): lax.ppermute(tail, axis, [(i, (i + 1) % count) for i in range(ends)])  22.3 us
    ppermute x12, starting transfers between devices, extended(): lax.ppermute(head, axis, [((i + 1) % count, i) for i in range(ends)])  20 us
    ppermute x12, waiting for transfers between devices, extended(): lax.ppermute(tail, axis, [(i, (i + 1) % count) for i in range(ends)])  19 us
    all_gather x4, blocking collectives, interface_sum(): lax.all_gather(edge_values, 'gx', axis=0, tiled=True)  18.4 us
    ppermute x12, waiting for transfers between devices, extended(): lax.ppermute(head, axis, [((i + 1) % count, i) for i in range(ends)])  10.4 us
    all_gather x1, blocking collectives, local(): every_inv = lax.all_gather(inverse_here, 'gx', axis=0, tiled=True)  5.17 us
    ppermute x2, local copies, waits for them, and re-layouts, extended(): lax.ppermute(head, axis, [((i + 1) % count, i) for i in range(ends)])  3.3 us
    slice x12, local copies, waits for them, and re-layouts, extended(): head = lax.slice_in_dim(cells, 0, width, axis=dim)  3.04 us
  transfers between devices with their start and end apart: 24, of which 9 were waited for; matrix products, arithmetic and copies ran while one was open for 15% of the time, Pallas kernels for 0%

commit v1 on v0

--- a/solution.py
+++ b/solution.py
@@ -6,6 +6,18 @@
 WIN = 8
 time_step = 0.15
 high = lax.Precision.HIGHEST
+
+
+def ring_product(array, axis, dim, product):
+    size, index = (lax.axis_size(axis), lax.axis_index(axis))
+    left = [(i, (i - 1) % size) for i in range(size)]
+    rows = array.shape[dim]
+    held = array
+    total = product(held, index * rows)
+    for step in range(1, size):
+        held = lax.ppermute(held, axis, left)
+        total = total + product(held, (index + step) % size * rows)
+    return total
 
 
 def extended(cells, sides, width, closed):
@@ -64,11 +76,16 @@
 
 
 def interface_sum(edge_values, weight_cols):
-    return jnp.einsum(
-        "ma,mcyz->acyz",
-        weight_cols,
-        lax.all_gather(edge_values, "gx", axis=0, tiled=True),
-        precision=high,
+    return ring_product(
+        edge_values,
+        "gx",
+        0,
+        lambda own_block, at: jnp.einsum(
+            "ma,mcyz->acyz",
+            lax.dynamic_slice_in_dim(weight_cols, at, own_block.shape[0], axis=0),
+            own_block,
+            precision=high,
+        ),
     )
 
 

time: 130 us -> 125 us (0.962)
  blocking collectives: 23.5 us -> 5.17 us
  starting transfers between devices: 42.3 us -> 50.8 us
  waiting for transfers between devices: 29.4 us -> 31.9 us
  matrix products: 9.75 us -> 11.2 us
    all_gather x4 -> x0, blocking collectives: 18.4 us -> none  [interface_sum(): lax.all_gather(edge_values, 'gx', axis=0, tiled=True)]
    ppermute x0 -> x4, starting transfers between devices: none -> 8.47 us  [ring_product(): held = lax.ppermute(held, axis, left)]
    ppermute x0 -> x4, waiting for transfers between devices: none -> 5.71 us  [ring_product(): held = lax.ppermute(held, axis, left)]
    ppermute x12, waiting for transfers between devices: 19 us -> 17.1 us  [extended(): lax.ppermute(tail, axis, [(i, (i + 1) % count) for i in range(ends)])]
    dot_general x4 -> x8, matrix products: 1.14 us -> 2.56 us  [interface_sum(): jnp.einsum('ma,mcyz->acyz', lax.dynamic_slice_in_dim(weight_cols, at, own...]
    ppermute x12, waiting for transfers between devices: 10.4 us -> 9.05 us  [extended(): lax.ppermute(head, axis, [((i + 1) % count, i) for i in range(ends)])]
  transfers between devices with their start and end apart: 24 -> 28, of which waited for: 9 -> 13; matrix products, arithmetic and copies ran while one was open for 15% -> 17% of each run, Pallas kernels for 0% -> 0%
where the time goes in v1:
time: 125 us; the launch traced here: 124 us
  starting transfers between devices  50.8 us (41%)
  waiting for transfers between devices  31.9 us (26%)
  local copies, waits for them, and re-layouts  18.1 us (14%)
  matrix products  11.2 us (9%)
  other arithmetic  5.95 us (5%)
  blocking collectives  5.17 us (4%)
    ppermute x12, starting transfers between devices, extended(): lax.ppermute(tail, axis, [(i, (i + 1) % count) for i in range(ends)])  22 us
    ppermute x12, starting transfers between devices, extended(): lax.ppermute(head, axis, [((i + 1) % count, i) for i in range(ends)])  20.3 us
    ppermute x12, waiting for transfers between devices, extended(): lax.ppermute(tail, axis, [(i, (i + 1) % count) for i in range(ends)])  17.1 us
    ppermute x12, waiting for transfers between devices, extended(): lax.ppermute(head, axis, [((i + 1) % count, i) for i in range(ends)])  9.05 us
    ppermute x4, starting transfers between devices, ring_product(): held = lax.ppermute(held, axis, left)  8.47 us
    ppermute x4, waiting for transfers between devices, ring_product(): held = lax.ppermute(held, axis, left)  5.71 us
    all_gather x1, blocking collectives, local(): every_inv = lax.all_gather(inverse_here, 'gx', axis=0, tiled=True)  5.17 us
    ppermute x2, local copies, waits for them, and re-layouts, extended(): lax.ppermute(head, axis, [((i + 1) % count, i) for i in range(ends)])  3.3 us
  transfers between devices with their start and end apart: 28, of which 13 were waited for; matrix products, arithmetic and copies ran while one was open for 17% of the time, Pallas kernels for 0%

profile of v1, /device:TPU:0, one launch (start us, length us, event | category | flops | bytes accessed | tf_op | source)
XLA Modules:
  0.0 123.9 jit_solution(15473751895877319537)
XLA Ops:
  0.0 1.0 copy.82
  1.0 0.5 collective-permute-start.4
  1.6 2.0 %collective-permute-start.3 = (f32[3,16,3,128]{3,1,2,0:T(8,128)S(1)}, f32[3,16,3,128]{3,1,2,0:T(8,128)S(1)}, u32[]{:S(2)}, u32[]{:S(2)}) collective-permute-start(f32[3,16,3,128]{3,1,2,0:T(8,128)S(1)} %get-tuple-element.51), channel_id=1, source_target_pairs={{4,0},{8,4},{12,8},{0,12},{5,1},{9,5},{13,9},{1,13},{6,2},{10,6},{... | collective-permute-start | bytes 221192 | tf_op jit(solution)/shard_map/ppermute | solution.py:33
  3.6 4.2 %collective-permute-start.1 = (f32[3,2,8,128]{3,1,2,0:T(2,128)S(1)}, f32[3,2,8,128]{3,1,2,0:T(2,128)S(1)}, u32[]{:S(2)}, u32[]{:S(2)}) collective-permute-start(f32[3,2,8,128]{3,1,2,0:T(2,128)S(1)} %get-tuple-element.44), channel_id=1, source_target_pairs={{0,16},{1,17},{2,18},{3,19},{4,20},{5,21},{6,22},{7,23},{8,24},{9,... | collective-permute-start | bytes 73736 | tf_op jit(solution)/shard_map/ppermute | solution.py:31
  7.8 1.3 %collective-permute-start = (f32[3,2,8,128]{3,1,2,0:T(2,128)S(1)}, f32[3,2,8,128]{3,1,2,0:T(2,128)S(1)}, u32[]{:S(2)}, u32[]{:S(2)}) collective-permute-start(f32[3,2,8,128]{3,1,2,0:T(2,128)S(1)} %get-tuple-element.43), channel_id=1, source_target_pairs={{16,0},{17,1},{18,2},{19,3},{20,4},{21,5},{22,6},{23,7},{24,8},{25... | collective-permute-start | bytes 73736 | tf_op jit(solution)/shard_map/ppermute | solution.py:33
  9.1 1.0 slice_convert_fusion
  10.1 0.6 copy.104
  10.8 0.6 copy.105
  12.1 5.2 %all-gather = f32[8,1,1,16,16]{4,3,2,1,0:T(8,128)S(1)} all-gather(f32[4,1,1,16,16]{4,3,2,1,0:T(8,128)S(1)} %copy-done.4), channel_id=2, replica_groups=mesh['gx'=2,'gy'=4,'gz'=4] {'gx'}, dimensions={0}, use_global_device_ids=true | all-gather | bytes 12288 | tf_op jit(solution)/shard_map/all_gather | solution.py:156
  18.0 1.6 %collective-permute-start.6 = (f32[3,16,14,3]{3,1,2,0:T(8,128)S(1)}, f32[3,16,14,3]{3,1,2,0:T(8,128)S(1)}, u32[]{:S(2)}, u32[]{:S(2)}) collective-permute-start(f32[3,16,14,3]{3,1,2,0:T(8,128)S(1)} %get-tuple-element.20), channel_id=1, source_target_pairs={{0,1},{1,2},{2,3},{3,0},{4,5},{5,6},{6,7},{7,4},{8,9},{9,10},{10,1... | collective-permute-start | bytes 24200 | tf_op jit(solution)/shard_map/ppermute | solution.py:31
  19.6 2.2 %collective-permute-start.5 = (f32[3,16,14,3]{3,1,2,0:T(8,128)S(1)}, f32[3,16,14,3]{3,1,2,0:T(8,128)S(1)}, u32[]{:S(2)}, u32[]{:S(2)}) collective-permute-start(f32[3,16,14,3]{3,1,2,0:T(8,128)S(1)} %get-tuple-element.19), channel_id=1, source_target_pairs={{1,0},{2,1},{3,2},{0,3},{5,4},{6,5},{7,6},{4,7},{9,8},{10,9},{11,1... | collective-permute-start | bytes 24200 | tf_op jit(solution)/shard_map/ppermute | solution.py:33
  22.6 2.1 %collective-permute-start.2 = (f32[2,3,8,128]{3,0,2,1:T(2,128)S(1)}, f32[2,3,8,128]{3,0,2,1:T(2,128)S(1)}, u32[]{:S(2)}, u32[]{:S(2)}) collective-permute-start(f32[2,3,8,128]{3,0,2,1:T(2,128)S(1)} %convolution_bitcast_fusion.6), channel_id=1, source_target_pairs={{0,16},{16,0},{1,17},{17,1},{2,18},{18,2},{3,19},{19,3},{4,20},{20... | collective-permute-start | bytes 73736 | tf_op jit(solution)/shard_map/ppermute | solution.py:18
  25.0 1.5 %collective-permute-done.2 = f32[2,3,8,128]{3,0,2,1:T(2,128)S(1)} collective-permute-done((f32[2,3,8,128]{3,0,2,1:T(2,128)S(1)}, f32[2,3,8,128]{3,0,2,1:T(2,128)S(1)}, u32[]{:S(2)}, u32[]{:S(2)}) %collective-permute-start.2) | collective-permute-done | bytes 24608 | tf_op jit(solution)/shard_map/ppermute | solution.py:18
  26.8 4.0 %collective-permute-done.6 = f32[3,16,14,3]{3,1,2,0:T(8,128)S(1)} collective-permute-done((f32[3,16,14,3]{3,1,2,0:T(8,128)S(1)}, f32[3,16,14,3]{3,1,2,0:T(8,128)S(1)}, u32[]{:S(2)}, u32[]{:S(2)}) %collective-permute-start.6) | collective-permute-done | bytes 8096 | tf_op jit(solution)/shard_map/ppermute | solution.py:31
  30.8 4.3 %collective-permute-done.5 = f32[3,16,14,3]{3,1,2,0:T(8,128)S(1)} collective-permute-done((f32[3,16,14,3]{3,1,2,0:T(8,128)S(1)}, f32[3,16,14,3]{3,1,2,0:T(8,128)S(1)}, u32[]{:S(2)}, u32[]{:S(2)}) %collective-permute-start.5) | collective-permute-done | bytes 8096 | tf_op jit(solution)/shard_map/ppermute | solution.py:33
  35.1 0.8 fusion.90
  36.2 0.8 reshape.79
  37.1 3.7 %collective-permute-start.8 = (f32[3,2,8,128]{3,1,2,0:T(2,128)S(1)}, f32[3,2,8,128]{3,1,2,0:T(2,128)S(1)}, u32[]{:S(2)}, u32[]{:S(2)}) collective-permute-start(f32[3,2,8,128]{3,1,2,0:T(2,128)S(1)} %get-tuple-element.42), channel_id=1, source_target_pairs={{0,16},{1,17},{2,18},{3,19},{4,20},{5,21},{6,22},{7,23},{8,24},{9,... | collective-permute-start | bytes 73736 | tf_op jit(solution)/shard_map/ppermute | solution.py:31
  40.7 1.3 %collective-permute-start.7 = (f32[3,2,8,128]{3,1,2,0:T(2,128)S(1)}, f32[3,2,8,128]{3,1,2,0:T(2,128)S(1)}, u32[]{:S(2)}, u32[]{:S(2)}) collective-permute-start(f32[3,2,8,128]{3,1,2,0:T(2,128)S(1)} %get-tuple-element.41), channel_id=1, source_target_pairs={{16,0},{17,1},{18,2},{19,3},{20,4},{21,5},{22,6},{23,7},{24,8},{25... | collective-permute-start | bytes 73736 | tf_op jit(solution)/shard_map/ppermute | solution.py:33
  42.0 0.5 reduce_sum.39
  42.8 0.5 broadcast_in_dim.19
  43.3 0.8 div.55
  44.1 1.7 %collective-permute-start.10 = (f32[3,16,3,128]{3,1,2,0:T(8,128)S(1)}, f32[3,16,3,128]{3,1,2,0:T(8,128)S(1)}, u32[]{:S(2)}, u32[]{:S(2)}) collective-permute-start(f32[3,16,3,128]{3,1,2,0:T(8,128)S(1)} %get-tuple-element.37), channel_id=1, source_target_pairs={{4,0},{8,4},{12,8},{0,12},{5,1},{9,5},{13,9},{1,13},{6,2},{10,6},{... | collective-permute-start | bytes 221192 | tf_op jit(solution)/shard_map/ppermute | solution.py:33
  45.9 0.6 collective-permute-done.7
  47.1 2.1 %collective-permute-start.9 = (f32[2,3,8,128]{3,0,2,1:T(2,128)S(1)}, f32[2,3,8,128]{3,0,2,1:T(2,128)S(1)}, u32[]{:S(2)}, u32[]{:S(2)}) collective-permute-start(f32[2,3,8,128]{3,0,2,1:T(2,128)S(1)} %convolution_bitcast_fusion.5), channel_id=1, source_target_pairs={{0,16},{16,0},{1,17},{17,1},{2,18},{18,2},{3,19},{19,3},{4,20},{20... | collective-permute-start | bytes 73736 | tf_op jit(solution)/shard_map/ppermute | solution.py:18
  49.5 1.5 %collective-permute-done.9 = f32[2,3,8,128]{3,0,2,1:T(2,128)S(1)} collective-permute-done((f32[2,3,8,128]{3,0,2,1:T(2,128)S(1)}, f32[2,3,8,128]{3,0,2,1:T(2,128)S(1)}, u32[]{:S(2)}, u32[]{:S(2)}) %collective-permute-start.9) | collective-permute-done | bytes 24608 | tf_op jit(solution)/shard_map/ppermute | solution.py:18
  51.6 1.2 collective-permute-start.13
  52.8 2.7 %collective-permute-start.12 = (f32[3,16,14,3]{3,1,2,0:T(8,128)S(1)}, f32[3,16,14,3]{3,1,2,0:T(8,128)S(1)}, u32[]{:S(2)}, u32[]{:S(2)}) collective-permute-start(f32[3,16,14,3]{3,1,2,0:T(8,128)S(1)} %get-tuple-element.17), channel_id=1, source_target_pairs={{1,0},{2,1},{3,2},{0,3},{5,4},{6,5},{7,6},{4,7},{9,8},{10,9},{11,1... | collective-permute-start | bytes 24200 | tf_op jit(solution)/shard_map/ppermute | solution.py:33
  55.8 8.5 %collective-permute-done.13 = f32[3,16,14,3]{3,1,2,0:T(8,128)S(1)} collective-permute-done((f32[3,16,14,3]{3,1,2,0:T(8,128)S(1)}, f32[3,16,14,3]{3,1,2,0:T(8,128)S(1)}, u32[]{:S(2)}, u32[]{:S(2)}) %collective-permute-start.13) | collective-permute-done | bytes 8096 | tf_op jit(solution)/shard_map/ppermute | solution.py:31
  64.4 3.5 %collective-permute-done.12 = f32[3,16,14,3]{3,1,2,0:T(8,128)S(1)} collective-permute-done((f32[3,16,14,3]{3,1,2,0:T(8,128)S(1)}, f32[3,16,14,3]{3,1,2,0:T(8,128)S(1)}, u32[]{:S(2)}, u32[]{:S(2)}) %collective-permute-start.12) | collective-permute-done | bytes 8096 | tf_op jit(solution)/shard_map/ppermute | solution.py:33
  67.9 0.8 fusion.102
  68.7 0.8 reshape.77
  69.5 0.5 reduce_sum.38
  70.8 0.8 div.50
  72.9 1.8 %collective-permute-start.14 = (f32[2,3,8,128]{3,0,2,1:T(2,128)S(1)}, f32[2,3,8,128]{3,0,2,1:T(2,128)S(1)}, u32[]{:S(2)}, u32[]{:S(2)}) collective-permute-start(f32[2,3,8,128]{3,0,2,1:T(2,128)S(1)} %convolution_bitcast_fusion.4), channel_id=1, source_target_pairs={{0,16},{16,0},{1,17},{17,1},{2,18},{18,2},{3,19},{19,3},{4,20},{20... | collective-permute-start | bytes 73736 | tf_op jit(solution)/shard_map/ppermute | solution.py:18
  74.8 0.5 collective-permute-start.18
  75.3 1.5 %collective-permute-done.14 = f32[2,3,8,128]{3,0,2,1:T(2,128)S(1)} collective-permute-done((f32[2,3,8,128]{3,0,2,1:T(2,128)S(1)}, f32[2,3,8,128]{3,0,2,1:T(2,128)S(1)}, u32[]{:S(2)}, u32[]{:S(2)}) %collective-permute-start.14) | collective-permute-done | bytes 24608 | tf_op jit(solution)/shard_map/ppermute | solution.py:18
  77.6 3.7 %collective-permute-start.16 = (f32[3,2,8,128]{3,1,2,0:T(2,128)S(1)}, f32[3,2,8,128]{3,1,2,0:T(2,128)S(1)}, u32[]{:S(2)}, u32[]{:S(2)}) collective-permute-start(f32[3,2,8,128]{3,1,2,0:T(2,128)S(1)} %get-tuple-element.34), channel_id=1, source_target_pairs={{0,16},{1,17},{2,18},{3,19},{4,20},{5,21},{6,22},{7,23},{8,24},{9,... | collective-permute-start | bytes 73736 | tf_op jit(solution)/shard_map/ppermute | solution.py:31
  81.2 1.5 %collective-permute-start.15 = (f32[3,2,8,128]{3,1,2,0:T(2,128)S(1)}, f32[3,2,8,128]{3,1,2,0:T(2,128)S(1)}, u32[]{:S(2)}, u32[]{:S(2)}) collective-permute-start(f32[3,2,8,128]{3,1,2,0:T(2,128)S(1)} %get-tuple-element.33), channel_id=1, source_target_pairs={{16,0},{17,1},{18,2},{19,3},{20,4},{21,5},{22,6},{23,7},{24,8},{25... | collective-permute-start | bytes 73736 | tf_op jit(solution)/shard_map/ppermute | solution.py:33
  83.1 0.7 copy.97
  83.8 0.8 collective-permute-start.20
  84.6 0.7 copy.95
  85.3 3.1 %collective-permute-start.19 = (f32[6,16,14,3]{2,1,3,0:T(8,128)S(1)}, f32[6,16,14,3]{2,1,3,0:T(8,128)}, u32[]{:S(2)}, u32[]{:S(2)}) collective-permute-start(f32[6,16,14,3]{2,1,3,0:T(8,128)S(1)} %copy.95), channel_id=1, source_target_pairs={{1,0},{2,1},{3,2},{0,3},{5,4},{6,5},{7,6},{4,7},{9,8},{10,9},{11,1... | collective-permute-start | bytes 48392 | tf_op jit(solution)/shard_map/ppermute | solution.py:33
  88.4 1.1 pad_maximum_fusion.2
  89.5 1.9 %collective-permute-done.20 = f32[6,16,14,3]{2,1,3,0:T(8,128)S(1)} collective-permute-done((f32[6,16,14,3]{2,1,3,0:T(8,128)S(1)}, f32[6,16,14,3]{2,1,3,0:T(8,128)S(1)}, u32[]{:S(2)}, u32[]{:S(2)}) %collective-permute-start.20) | collective-permute-done | bytes 16160 | tf_op jit(solution)/shard_map/ppermute | solution.py:31
  91.4 0.8 copy.98
  92.5 1.7 %copy.96 = f32[6,16,14,3]{3,1,2,0:T(8,128)S(1)} copy(f32[6,16,14,3]{2,1,3,0:T(8,128)} %collective-permute-done.19) | data formatting | bytes 32256 | tf_op jit(solution)/shard_map/ppermute | solution.py:33
  94.2 0.6 copy-done.14
  94.8 2.1 %broadcast_multiply_fusion.1 = (f32[3,16,8,128]{3,1,2,0:T(8,128)S(1)}, f32[3,16,8,128]{3,1,2,0:T(8,128)S(1)}, f32[3,16,8,128]{3,1,2,0:T(8,128)S(1)}) fusion(f32[16,8,128]{2,0,1:T(8,128)S(1)} %copy-done.3, f32[16,8,128]{2,0,1:T(8,128)} %copy.105, s32[8]{0:T(128)S(1)} %copy-done.10, pred[8]{0:T(512)(128)(4,1)S(1)} %copy-done.12, ...), kind=kOutput, calls=%fused_computation.213 | convolution fusion | flops 7471360 | bytes 3161640 | tf_op jit(solution)/shard_map/sx,scyz->cxyz/dot_general | solution.py:154
  97.9 2.4 %collective-permute-start.21 = (f32[2,3,8,128]{3,0,2,1:T(2,128)S(1)}, f32[2,3,8,128]{3,0,2,1:T(2,128)S(1)}, u32[]{:S(2)}, u32[]{:S(2)}) collective-permute-start(f32[2,3,8,128]{3,0,2,1:T(2,128)S(1)} %convolution_bitcast_fusion.3), channel_id=1, source_target_pairs={{0,16},{16,0},{1,17},{17,1},{2,18},{18,2},{3,19},{19,3},{4,20},{20... | collective-permute-start | bytes 73736 | tf_op jit(solution)/shard_map/ppermute | solution.py:18
  100.4 0.5 collective-permute-start.25
  100.9 1.2 collective-permute-done.21
  102.9 0.7 fusion.184
  103.5 4.5 %collective-permute-start.23 = (f32[3,2,8,128]{3,1,2,0:T(2,128)}, f32[3,2,8,128]{3,1,2,0:T(2,128)}, u32[]{:S(2)}, u32[]{:S(2)}) collective-permute-start(f32[3,2,8,128]{3,1,2,0:T(2,128)} %get-tuple-element.27), channel_id=1, source_target_pairs={{0,16},{1,17},{2,18},{3,19},{4,20},{5,21},{6,22},{7,23},{8,24},{9,... | collective-permute-start | bytes 73736 | tf_op jit(solution)/shard_map/ppermute | solution.py:31
  108.1 1.3 %collective-permute-start.22 = (f32[3,2,8,128]{3,1,2,0:T(2,128)}, f32[3,2,8,128]{3,1,2,0:T(2,128)}, u32[]{:S(2)}, u32[]{:S(2)}) collective-permute-start(f32[3,2,8,128]{3,1,2,0:T(2,128)} %get-tuple-element.26), channel_id=1, source_target_pairs={{16,0},{17,1},{18,2},{19,3},{20,4},{21,5},{22,6},{23,7},{24,8},{25... | collective-permute-start | bytes 73736 | tf_op jit(solution)/shard_map/ppermute | solution.py:33
  109.7 1.4 %copy.108 = f32[6,16,14,3]{2,1,3,0:T(8,128)} copy(f32[6,16,14,3]{3,1,2,0:T(8,128)S(1)} %get-tuple-element.6) | data formatting | bytes 32256 | tf_op jit(solution)/shard_map/slice | solution.py:28
  111.1 0.8 collective-permute-start.27
  111.9 0.7 copy.106
  112.7 3.0 %collective-permute-start.26 = (f32[6,16,14,3]{2,1,3,0:T(8,128)S(1)}, f32[6,16,14,3]{2,1,3,0:T(8,128)}, u32[]{:S(2)}, u32[]{:S(2)}) collective-permute-start(f32[6,16,14,3]{2,1,3,0:T(8,128)S(1)} %copy.106), channel_id=1, source_target_pairs={{1,0},{2,1},{3,2},{0,3},{5,4},{6,5},{7,6},{4,7},{9,8},{10,9},{11,1... | collective-permute-start | bytes 48392 | tf_op jit(solution)/shard_map/ppermute | solution.py:33
  115.8 2.6 %collective-permute-done.27 = f32[6,16,14,3]{2,1,3,0:T(8,128)S(1)} collective-permute-done((f32[6,16,14,3]{2,1,3,0:T(8,128)}, f32[6,16,14,3]{2,1,3,0:T(8,128)S(1)}, u32[]{:S(2)}, u32[]{:S(2)}) %collective-permute-start.27) | collective-permute-done | bytes 16160 | tf_op jit(solution)/shard_map/ppermute | solution.py:31
  118.4 0.8 copy.109
  119.5 1.7 %copy.107 = f32[6,16,14,3]{3,1,2,0:T(8,128)S(1)} copy(f32[6,16,14,3]{2,1,3,0:T(8,128)} %collective-permute-done.26) | data formatting | bytes 32256 | tf_op jit(solution)/shard_map/ppermute | solution.py:33
  121.2 2.0 %fusion.30 = f32[3,16,8,128]{3,1,2,0:T(8,128)S(1)} fusion(f32[3,16,8,128]{3,1,2,0:T(8,128)S(1)} %get-tuple-element.62, f32[3,2,8,128]{3,1,2,0:T(2,128)} %collective-permute-done.23, f32[3,16,8,128]{3,1,2,0:T(8,128)} %copy-done.2, f32[3,2,8,128]{3,1,2,0:T(2,128)} %collective-permute-done.22, f32[6,16,14,3]{3,1,2,0:T(8,128)S(1)} %copy.109, ...), kind=kLoop, calls=%fused_computation.77 | loop fusion | flops 2654208 | bytes 2735616 | tf_op jit(solution)/shard_map/add | solution.py:181
  123.2 0.7 copy.111
  (120 shorter events, 11.0 us)
Async XLA Ops:
  0.0 22.0 %copy-start = (f32[16,16]{1,0:T(8,128)S(1)}, f32[16,16]{1,0:T(8,128)}, u32[]{:S(2)}) copy-start(f32[16,16]{1,0:T(8,128)} %param.11) | copy-start | bytes 3076
  0.0 11.4 %copy-start.13 = (s32[8]{0:T(128)S(1)}, s32[8]{0:T(128)}, u32[]{:S(2)}) copy-start(s32[8]{0:T(128)} %param.15) | copy-start | bytes 100
  1.0 10.9 %copy-start.16 = (s32[8]{0:T(128)S(1)}, s32[8]{0:T(128)}, u32[]{:S(2)}) copy-start(s32[8]{0:T(128)} %param.16) | copy-start | bytes 100
  1.0 11.1 %copy-start.4 = (f32[4,1,1,16,16]{4,3,2,1,0:T(8,128)S(1)}, f32[4,1,1,16,16]{4,3,2,1,0:T(8,128)}, u32[]{:S(2)}) copy-start(f32[4,1,1,16,16]{4,3,2,1,0:T(8,128)} %param.17) | copy-start | bytes 12292
  1.0 16.6 %collective-permute-start.4 = (f32[3,16,3,128]{3,1,2,0:T(8,128)S(1)}, f32[3,16,3,128]{3,1,2,0:T(8,128)S(1)}, u32[]{:S(2)}, u32[]{:S(2)}) collective-permute-start(f32[3,16,3,128]{3,1,2,0:T(8,128)S(1)} %get-tuple-element.52), channel_id=1, source_target_pairs={{0,4},{4,8},{8,12},{12,0},{1,5},{5,9},{9,13},{13,1},{2,6},{6,10},{... | collective-permute-start | bytes 221192 | tf_op jit(solution)/shard_map/ppermute | solution.py:31
  1.6 16.2 %collective-permute-start.3 = (f32[3,16,3,128]{3,1,2,0:T(8,128)S(1)}, f32[3,16,3,128]{3,1,2,0:T(8,128)S(1)}, u32[]{:S(2)}, u32[]{:S(2)}) collective-permute-start(f32[3,16,3,128]{3,1,2,0:T(8,128)S(1)} %get-tuple-element.51), channel_id=1, source_target_pairs={{4,0},{8,4},{12,8},{0,12},{5,1},{9,5},{13,9},{1,13},{6,2},{10,6},{... | collective-permute-start | bytes 221192 | tf_op jit(solution)/shard_map/ppermute | solution.py:33
  3.6 18.3 %collective-permute-start.1 = (f32[3,2,8,128]{3,1,2,0:T(2,128)S(1)}, f32[3,2,8,128]{3,1,2,0:T(2,128)S(1)}, u32[]{:S(2)}, u32[]{:S(2)}) collective-permute-start(f32[3,2,8,128]{3,1,2,0:T(2,128)S(1)} %get-tuple-element.44), channel_id=1, source_target_pairs={{0,16},{1,17},{2,18},{3,19},{4,20},{5,21},{6,22},{7,23},{8,24},{9,... | collective-permute-start | bytes 73736 | tf_op jit(solution)/shard_map/ppermute | solution.py:31
  7.8 14.1 %collective-permute-start = (f32[3,2,8,128]{3,1,2,0:T(2,128)S(1)}, f32[3,2,8,128]{3,1,2,0:T(2,128)S(1)}, u32[]{:S(2)}, u32[]{:S(2)}) collective-permute-start(f32[3,2,8,128]{3,1,2,0:T(2,128)S(1)} %get-tuple-element.43), channel_id=1, source_target_pairs={{16,0},{17,1},{18,2},{19,3},{20,4},{21,5},{22,6},{23,7},{24,8},{25... | collective-permute-start | bytes 73736 | tf_op jit(solution)/shard_map/ppermute | solution.py:33
  10.0 7.7 %copy-start.1 = (f32[3,16,8,128]{3,2,1,0:T(8,128)S(1)}, f32[3,16,8,128]{3,2,1,0:T(8,128)}, u32[]{:S(2)}) copy-start(f32[3,16,8,128]{3,2,1,0:T(8,128)} %param.9) | copy-start | bytes 589828
  11.8 59.8 %copy-start.11 = (pred[8]{0:T(512)(128)(4,1)}, pred[8]{0:T(512)(128)(4,1)S(1)}, u32[]{:S(2)}) copy-start(pred[8]{0:T(512)(128)(4,1)S(1)} %broadcast_compare_fusion.1) | copy-start | bytes 28
  17.7 53.9 %copy-start.9 = (s32[8]{0:T(128)}, s32[8]{0:T(128)S(1)}, u32[]{:S(2)}) copy-start(s32[8]{0:T(128)S(1)} %select_reduce_fusion) | copy-start | bytes 100
  17.8 4.6 %copy-start.6 = (f32[2,16]{1,0:T(2,128)S(1)}, f32[2,16]{1,0:T(2,128)}, u32[]{:S(2)}) copy-start(f32[2,16]{1,0:T(2,128)} %param.12) | copy-start | bytes 388
  17.8 6.9 %copy-start.7 = (f32[4,4]{1,0:T(4,128)S(1)}, f32[4,4]{1,0:T(4,128)}, u32[]{:S(2)}) copy-start(f32[4,4]{1,0:T(4,128)} %param.14) | copy-start | bytes 196
  17.8 17.3 %copy-start.5 = (f32[16,2]{0,1:T(2,128)S(1)}, f32[16,2]{0,1:T(2,128)}, u32[]{:S(2)}) copy-start(f32[16,2]{0,1:T(2,128)} %param.13) | copy-start | bytes 388
  18.0 12.8 %collective-permute-start.6 = (f32[3,16,14,3]{3,1,2,0:T(8,128)S(1)}, f32[3,16,14,3]{3,1,2,0:T(8,128)S(1)}, u32[]{:S(2)}, u32[]{:S(2)}) collective-permute-start(f32[3,16,14,3]{3,1,2,0:T(8,128)S(1)} %get-tuple-element.20), channel_id=1, source_target_pairs={{0,1},{1,2},{2,3},{3,0},{4,5},{5,6},{6,7},{7,4},{8,9},{9,10},{10,1... | collective-permute-start | bytes 24200 | tf_op jit(solution)/shard_map/ppermute | solution.py:31
  19.6 15.5 %collective-permute-start.5 = (f32[3,16,14,3]{3,1,2,0:T(8,128)S(1)}, f32[3,16,14,3]{3,1,2,0:T(8,128)S(1)}, u32[]{:S(2)}, u32[]{:S(2)}) collective-permute-start(f32[3,16,14,3]{3,1,2,0:T(8,128)S(1)} %get-tuple-element.19), channel_id=1, source_target_pairs={{1,0},{2,1},{3,2},{0,3},{5,4},{6,5},{7,6},{4,7},{9,8},{10,9},{11,1... | collective-permute-start | bytes 24200 | tf_op jit(solution)/shard_map/ppermute | solution.py:33
  22.6 3.9 %collective-permute-start.2 = (f32[2,3,8,128]{3,0,2,1:T(2,128)S(1)}, f32[2,3,8,128]{3,0,2,1:T(2,128)S(1)}, u32[]{:S(2)}, u32[]{:S(2)}) collective-permute-start(f32[2,3,8,128]{3,0,2,1:T(2,128)S(1)} %convolution_bitcast_fusion.6), channel_id=1, source_target_pairs={{0,16},{16,0},{1,17},{17,1},{2,18},{18,2},{3,19},{19,3},{4,20},{20... | collective-permute-start | bytes 73736 | tf_op jit(solution)/shard_map/ppermute | solution.py:18
  37.1 8.8 %collective-permute-start.8 = (f32[3,2,8,128]{3,1,2,0:T(2,128)S(1)}, f32[3,2,8,128]{3,1,2,0:T(2,128)S(1)}, u32[]{:S(2)}, u32[]{:S(2)}) collective-permute-start(f32[3,2,8,128]{3,1,2,0:T(2,128)S(1)} %get-tuple-element.42), channel_id=1, source_target_pairs={{0,16},{1,17},{2,18},{3,19},{4,20},{5,21},{6,22},{7,23},{8,24},{9,... | collective-permute-start | bytes 73736 | tf_op jit(solution)/shard_map/ppermute | solution.py:31
  40.7 5.7 %collective-permute-start.7 = (f32[3,2,8,128]{3,1,2,0:T(2,128)S(1)}, f32[3,2,8,128]{3,1,2,0:T(2,128)S(1)}, u32[]{:S(2)}, u32[]{:S(2)}) collective-permute-start(f32[3,2,8,128]{3,1,2,0:T(2,128)S(1)} %get-tuple-element.41), channel_id=1, source_target_pairs={{16,0},{17,1},{18,2},{19,3},{20,4},{21,5},{22,6},{23,7},{24,8},{25... | collective-permute-start | bytes 73736 | tf_op jit(solution)/shard_map/ppermute | solution.py:33
  44.1 7.3 %collective-permute-start.11 = (f32[3,16,3,128]{3,1,2,0:T(8,128)S(1)}, f32[3,16,3,128]{3,1,2,0:T(8,128)S(1)}, u32[]{:S(2)}, u32[]{:S(2)}) collective-permute-start(f32[3,16,3,128]{3,1,2,0:T(8,128)S(1)} %get-tuple-element.38), channel_id=1, source_target_pairs={{0,4},{4,8},{8,12},{12,0},{1,5},{5,9},{9,13},{13,1},{2,6},{6,10},{... | collective-permute-start | bytes 221192 | tf_op jit(solution)/shard_map/ppermute | solution.py:31
  44.1 7.2 %collective-permute-start.10 = (f32[3,16,3,128]{3,1,2,0:T(8,128)S(1)}, f32[3,16,3,128]{3,1,2,0:T(8,128)S(1)}, u32[]{:S(2)}, u32[]{:S(2)}) collective-permute-start(f32[3,16,3,128]{3,1,2,0:T(8,128)S(1)} %get-tuple-element.37), channel_id=1, source_target_pairs={{4,0},{8,4},{12,8},{0,12},{5,1},{9,5},{13,9},{1,13},{6,2},{10,6},{... | collective-permute-start | bytes 221192 | tf_op jit(solution)/shard_map/ppermute | solution.py:33
  47.1 3.9 %collective-permute-start.9 = (f32[2,3,8,128]{3,0,2,1:T(2,128)S(1)}, f32[2,3,8,128]{3,0,2,1:T(2,128)S(1)}, u32[]{:S(2)}, u32[]{:S(2)}) collective-permute-start(f32[2,3,8,128]{3,0,2,1:T(2,128)S(1)} %convolution_bitcast_fusion.5), channel_id=1, source_target_pairs={{0,16},{16,0},{1,17},{17,1},{2,18},{18,2},{3,19},{19,3},{4,20},{20... | collective-permute-start | bytes 73736 | tf_op jit(solution)/shard_map/ppermute | solution.py:18
  51.6 12.8 %collective-permute-start.13 = (f32[3,16,14,3]{3,1,2,0:T(8,128)S(1)}, f32[3,16,14,3]{3,1,2,0:T(8,128)S(1)}, u32[]{:S(2)}, u32[]{:S(2)}) collective-permute-start(f32[3,16,14,3]{3,1,2,0:T(8,128)S(1)} %get-tuple-element.18), channel_id=1, source_target_pairs={{0,1},{1,2},{2,3},{3,0},{4,5},{5,6},{6,7},{7,4},{8,9},{9,10},{10,1... | collective-permute-start | bytes 24200 | tf_op jit(solution)/shard_map/ppermute | solution.py:31
  52.8 15.1 %collective-permute-start.12 = (f32[3,16,14,3]{3,1,2,0:T(8,128)S(1)}, f32[3,16,14,3]{3,1,2,0:T(8,128)S(1)}, u32[]{:S(2)}, u32[]{:S(2)}) collective-permute-start(f32[3,16,14,3]{3,1,2,0:T(8,128)S(1)} %get-tuple-element.17), channel_id=1, source_target_pairs={{1,0},{2,1},{3,2},{0,3},{5,4},{6,5},{7,6},{4,7},{9,8},{10,9},{11,1... | collective-permute-start | bytes 24200 | tf_op jit(solution)/shard_map/ppermute | solution.py:33
  72.9 3.9 %collective-permute-start.14 = (f32[2,3,8,128]{3,0,2,1:T(2,128)S(1)}, f32[2,3,8,128]{3,0,2,1:T(2,128)S(1)}, u32[]{:S(2)}, u32[]{:S(2)}) collective-permute-start(f32[2,3,8,128]{3,0,2,1:T(2,128)S(1)} %convolution_bitcast_fusion.4), channel_id=1, source_target_pairs={{0,16},{16,0},{1,17},{17,1},{2,18},{18,2},{3,19},{19,3},{4,20},{20... | collective-permute-start | bytes 73736 | tf_op jit(solution)/shard_map/ppermute | solution.py:18
  74.8 8.0 %collective-permute-start.17 = (f32[6,16,3,128]{3,1,2,0:T(8,128)S(1)}, f32[6,16,3,128]{3,1,2,0:T(8,128)S(1)}, u32[]{:S(2)}, u32[]{:S(2)}) collective-permute-start(f32[6,16,3,128]{3,1,2,0:T(8,128)S(1)} %get-tuple-element.16), channel_id=1, source_target_pairs={{4,0},{8,4},{12,8},{0,12},{5,1},{9,5},{13,9},{1,13},{6,2},{10,6},{... | collective-permute-start | bytes 442376 | tf_op jit(solution)/shard_map/ppermute | solution.py:33
  74.8 7.9 %collective-permute-start.18 = (f32[6,16,3,128]{3,1,2,0:T(8,128)S(1)}, f32[6,16,3,128]{3,1,2,0:T(8,128)S(1)}, u32[]{:S(2)}, u32[]{:S(2)}) collective-permute-start(f32[6,16,3,128]{3,1,2,0:T(8,128)S(1)} %get-tuple-element.15), channel_id=1, source_target_pairs={{0,4},{4,8},{8,12},{12,0},{1,5},{5,9},{9,13},{13,1},{2,6},{6,10},{... | collective-permute-start | bytes 442376 | tf_op jit(solution)/shard_map/ppermute | solution.py:31
  77.6 16.6 %collective-permute-start.16 = (f32[3,2,8,128]{3,1,2,0:T(2,128)S(1)}, f32[3,2,8,128]{3,1,2,0:T(2,128)S(1)}, u32[]{:S(2)}, u32[]{:S(2)}) collective-permute-start(f32[3,2,8,128]{3,1,2,0:T(2,128)S(1)} %get-tuple-element.34), channel_id=1, source_target_pairs={{0,16},{1,17},{2,18},{3,19},{4,20},{5,21},{6,22},{7,23},{8,24},{9,... | collective-permute-start | bytes 73736 | tf_op jit(solution)/shard_map/ppermute | solution.py:31
  81.2 12.9 %collective-permute-start.15 = (f32[3,2,8,128]{3,1,2,0:T(2,128)S(1)}, f32[3,2,8,128]{3,1,2,0:T(2,128)S(1)}, u32[]{:S(2)}, u32[]{:S(2)}) collective-permute-start(f32[3,2,8,128]{3,1,2,0:T(2,128)S(1)} %get-tuple-element.33), channel_id=1, source_target_pairs={{16,0},{17,1},{18,2},{19,3},{20,4},{21,5},{22,6},{23,7},{24,8},{25... | collective-permute-start | bytes 73736 | tf_op jit(solution)/shard_map/ppermute | solution.py:33
  83.8 7.7 %collective-permute-start.20 = (f32[6,16,14,3]{2,1,3,0:T(8,128)S(1)}, f32[6,16,14,3]{2,1,3,0:T(8,128)S(1)}, u32[]{:S(2)}, u32[]{:S(2)}) collective-permute-start(f32[6,16,14,3]{2,1,3,0:T(8,128)S(1)} %copy.97), channel_id=1, source_target_pairs={{0,1},{1,2},{2,3},{3,0},{4,5},{5,6},{6,7},{7,4},{8,9},{9,10},{10,1... | collective-permute-start | bytes 48392 | tf_op jit(solution)/shard_map/ppermute | solution.py:31
  85.3 9.5 %copy-start.3 = (f32[16,8,128]{2,0,1:T(8,128)S(1)}, f32[16,8,128]{2,0,1:T(8,128)}, u32[]{:S(2)}) copy-start(f32[16,8,128]{2,0,1:T(8,128)} %copy.104) | copy-start | bytes 196612
  85.3 9.5 %copy-start.10 = (s32[8]{0:T(128)S(1)}, s32[8]{0:T(128)}, u32[]{:S(2)}) copy-start(s32[8]{0:T(128)} %copy-done.9) | copy-start | bytes 100
  85.3 9.5 %copy-start.12 = (pred[8]{0:T(512)(128)(4,1)S(1)}, pred[8]{0:T(512)(128)(4,1)}, u32[]{:S(2)}) copy-start(pred[8]{0:T(512)(128)(4,1)} %copy-done.11) | copy-start | bytes 28
  85.3 7.2 %collective-permute-start.19 = (f32[6,16,14,3]{2,1,3,0:T(8,128)S(1)}, f32[6,16,14,3]{2,1,3,0:T(8,128)}, u32[]{:S(2)}, u32[]{:S(2)}) collective-permute-start(f32[6,16,14,3]{2,1,3,0:T(8,128)S(1)} %copy.95), channel_id=1, source_target_pairs={{1,0},{2,1},{3,2},{0,3},{5,4},{6,5},{7,6},{4,7},{9,8},{10,9},{11,1... | collective-permute-start | bytes 48392 | tf_op jit(solution)/shard_map/ppermute | solution.py:33
  94.1 0.6 copy-start.14
  94.2 0.6 copy-start.15
  94.8 2.8 %copy-start.8 = (f32[4,4]{1,0:T(4,128)S(1)}, f32[4,4]{1,0:T(4,128)}, u32[]{:S(2)}) copy-start(f32[4,4]{1,0:T(4,128)} %param.14) | copy-start | bytes 196
  97.9 4.2 %collective-permute-start.21 = (f32[2,3,8,128]{3,0,2,1:T(2,128)S(1)}, f32[2,3,8,128]{3,0,2,1:T(2,128)S(1)}, u32[]{:S(2)}, u32[]{:S(2)}) collective-permute-start(f32[2,3,8,128]{3,0,2,1:T(2,128)S(1)} %convolution_bitcast_fusion.3), channel_id=1, source_target_pairs={{0,16},{16,0},{1,17},{17,1},{2,18},{18,2},{3,19},{19,3},{4,20},{20... | collective-permute-start | bytes 73736 | tf_op jit(solution)/shard_map/ppermute | solution.py:18
  100.4 9.0 %collective-permute-start.24 = (f32[6,16,3,128]{3,1,2,0:T(8,128)S(1)}, f32[6,16,3,128]{3,1,2,0:T(8,128)S(1)}, u32[]{:S(2)}, u32[]{:S(2)}) collective-permute-start(f32[6,16,3,128]{3,1,2,0:T(8,128)S(1)} %get-tuple-element.12), channel_id=1, source_target_pairs={{4,0},{8,4},{12,8},{0,12},{5,1},{9,5},{13,9},{1,13},{6,2},{10,6},{... | collective-permute-start | bytes 442376 | tf_op jit(solution)/shard_map/ppermute | solution.py:33
  100.4 9.0 %collective-permute-start.25 = (f32[6,16,3,128]{3,1,2,0:T(8,128)S(1)}, f32[6,16,3,128]{3,1,2,0:T(8,128)S(1)}, u32[]{:S(2)}, u32[]{:S(2)}) collective-permute-start(f32[6,16,3,128]{3,1,2,0:T(8,128)S(1)} %get-tuple-element.11), channel_id=1, source_target_pairs={{0,4},{4,8},{8,12},{12,0},{1,5},{5,9},{9,13},{13,1},{2,6},{6,10},{... | collective-permute-start | bytes 442376 | tf_op jit(solution)/shard_map/ppermute | solution.py:31
  102.9 9.8 %copy-start.2 = (f32[3,16,8,128]{3,1,2,0:T(8,128)}, f32[3,16,8,128]{3,1,2,0:T(8,128)S(1)}, u32[]{:S(2)}) copy-start(f32[3,16,8,128]{3,1,2,0:T(8,128)S(1)} %fusion.5) | copy-start | bytes 589828
  103.5 17.6 %collective-permute-start.23 = (f32[3,2,8,128]{3,1,2,0:T(2,128)}, f32[3,2,8,128]{3,1,2,0:T(2,128)}, u32[]{:S(2)}, u32[]{:S(2)}) collective-permute-start(f32[3,2,8,128]{3,1,2,0:T(2,128)} %get-tuple-element.27), channel_id=1, source_target_pairs={{0,16},{1,17},{2,18},{3,19},{4,20},{5,21},{6,22},{7,23},{8,24},{9,... | collective-permute-start | bytes 73736 | tf_op jit(solution)/shard_map/ppermute | solution.py:31
  108.1 13.1 %collective-permute-start.22 = (f32[3,2,8,128]{3,1,2,0:T(2,128)}, f32[3,2,8,128]{3,1,2,0:T(2,128)}, u32[]{:S(2)}, u32[]{:S(2)}) collective-permute-start(f32[3,2,8,128]{3,1,2,0:T(2,128)} %get-tuple-element.26), channel_id=1, source_target_pairs={{16,0},{17,1},{18,2},{19,3},{20,4},{21,5},{22,6},{23,7},{24,8},{25... | collective-permute-start | bytes 73736 | tf_op jit(solution)/shard_map/ppermute | solution.py:33
  111.1 7.3 %collective-permute-start.27 = (f32[6,16,14,3]{2,1,3,0:T(8,128)}, f32[6,16,14,3]{2,1,3,0:T(8,128)S(1)}, u32[]{:S(2)}, u32[]{:S(2)}) collective-permute-start(f32[6,16,14,3]{2,1,3,0:T(8,128)} %copy.108), channel_id=1, source_target_pairs={{0,1},{1,2},{2,3},{3,0},{4,5},{5,6},{6,7},{7,4},{8,9},{9,10},{10,1... | collective-permute-start | bytes 48392 | tf_op jit(solution)/shard_map/ppermute | solution.py:31
  112.7 6.9 %collective-permute-start.26 = (f32[6,16,14,3]{2,1,3,0:T(8,128)S(1)}, f32[6,16,14,3]{2,1,3,0:T(8,128)}, u32[]{:S(2)}, u32[]{:S(2)}) collective-permute-start(f32[6,16,14,3]{2,1,3,0:T(8,128)S(1)} %copy.106), channel_id=1, source_target_pairs={{1,0},{2,1},{3,2},{0,3},{5,4},{6,5},{7,6},{4,7},{9,8},{10,9},{11,1... | collective-permute-start | bytes 48392 | tf_op jit(solution)/shard_map/ppermute | solution.py:33
